TPU v7x, 256 devices: a whole 4x4x8 slice. The times are simulated.
256 devices in a mesh: pix: 16 (over y, x_hi, core), tm: 16 (over x_lo, z).
Axes of the slice: x: 4 (x_hi: 2, x_lo: 2; x = x_hi * 2 + x_lo), y: 4, z: 8, core: 2. Of those that a mesh axis runs over, the one named last changes fastest.
Arguments:
- raw_movie: float32 [128, 256, 8192], P('pix', None, 'tm'), may hold values from 0.05 to 2
- footprints: float32 [256, 32768], P('tm', 'pix'), may hold values from 0.05 to 1
- traces: float32 [256, 8192], P('pix', 'tm'), may hold values from 0.05 to 1
Outputs:
- denoised: float32 [128, 256, 8192], P('pix', None, 'tm')
- new_footprints: float32 [256, 32768], P('tm', 'pix')
- new_traces: float32 [256, 8192], P('pix', 'tm')
All inputs are finite; a program needn't handle non-finite values.
Results may differ from a plain program's by a relative error of at most 0.00013.
Values sent between devices are 32-bit elements; how exact they have to be, the bound alone decides.
A program may use at most 64 MiB of HBM per device.

v0:
```python
import jax
import jax.numpy as jnp
from jax import lax
from jax.sharding import PartitionSpec as P

edge_scale = 0.5
step_size = 0.24


def with_halo(cells, sides, width):
    for axis, dim in sides:
        count = lax.axis_size(axis)
        ends = count - 1
        head = lax.slice_in_dim(cells, 0, width, axis=dim)
        tail = lax.slice_in_dim(cells, cells.shape[dim] - width, cells.shape[dim], axis=dim)
        cells = jnp.concatenate(
            [
                lax.ppermute(tail, axis, [(i, (i + 1) % count) for i in range(ends)]),
                cells,
                lax.ppermute(head, axis, [((i + 1) % count, i) for i in range(ends)]),
            ],
            axis=dim,
        )
    return cells


def flux_term(change):
    return change / (1.0 + change / edge_scale * (change / edge_scale))


def substep(extended):
    middle = extended[1:-1]
    padded = jnp.pad(middle, ((0, 0), (1, 1), (0, 0)))
    summed = flux_term(extended[:-2] - middle) + flux_term(extended[2:] - middle)
    summed = summed + flux_term(padded[:, :-2] - middle) + flux_term(padded[:, 2:] - middle)
    return middle + step_size * summed


def matmul_hi(left, right):
    return jnp.dot(left, right, precision=lax.Precision.HIGHEST, preferred_element_type=jnp.float32)


def contract_last(left, right):
    return lax.dot_general(
        left,
        right,
        (((1,), (1,)), ((), ())),
        precision=lax.Precision.HIGHEST,
        preferred_element_type=jnp.float32,
    )


def body(raw_movie, footprints, traces):
    row_count = raw_movie.shape[0]
    col_count = raw_movie.shape[1]
    frame_count = raw_movie.shape[2]
    current = raw_movie
    for repeat in range(4):
        extended = with_halo(current, (("pix", 0),), 1)
        current = substep(extended)
    pixels = current.reshape(row_count * col_count, frame_count)
    foot_full = lax.all_gather(footprints, "tm", axis=0, tiled=True)
    trace_full = lax.all_gather(traces, "pix", axis=0, tiled=True)
    rank_block = traces.shape[0]
    rank_start = lax.axis_index("pix") * rank_block
    part = foot_full
    numerator = lax.psum_scatter(matmul_hi(part, pixels), "pix", scatter_dimension=0, tiled=True)
    gram = lax.psum(contract_last(foot_full, foot_full), "pix")
    gram_rows = lax.dynamic_slice_in_dim(gram, rank_start, rank_block, 0)
    new_traces = traces * numerator / matmul_hi(gram_rows, trace_full)
    new_full = lax.all_gather(new_traces, "pix", axis=0, tiled=True)
    foot_block = footprints.shape[0]
    foot_start = lax.axis_index("tm") * foot_block
    part = new_full
    foot_numerator = lax.psum_scatter(
        contract_last(part, pixels), "tm", scatter_dimension=0, tiled=True
    )
    trace_gram = lax.psum(contract_last(new_full, new_full), "tm")
    trace_rows = lax.dynamic_slice_in_dim(trace_gram, foot_start, foot_block, 0)
    new_footprints = footprints * foot_numerator / matmul_hi(trace_rows, foot_full)
    return (current, new_footprints, new_traces)


def solution(mesh):
    placed = (P("pix", None, "tm"), P("tm", "pix"), P("pix", "tm"))
    return jax.shard_map(
        body,
        mesh=mesh,
        in_specs=placed,
        out_specs=(P("pix", None, "tm"), P("tm", "pix"), P("pix", "tm")),
        check_vma=False,
    )
```

profile of v0, /device:TPU:8, one launch (start us, length us, event | category | flops | bytes accessed | tf_op | source)
XLA Modules:
  0.0 603.0 jit_solution(13072026490475913355)
XLA Ops:
  7.2 0.0 all-gather.2.cloned.1.call-start
  7.2 1.3 fusion.16
  8.5 1.9 collective-permute-start
  10.4 6.0 %collective-permute-start.1 = (f32[1,256,512]{2,1,0:T(8,128)S(1)}, f32[1,256,512]{2,1,0:T(8,128)S(1)}, u32[]{:S(2)}, u32[]{:S(2)}) collective-permute-start(f32[1,256,512]{2,1,0:T(8,128)S(1)} %get-tuple-element.13), channel_id=1, source_target_pairs={{16,0},{32,16},{48,32},{64,48},{80,64},{96,80},{112,96},{128,112},... | collective-permute-start | bytes 1572872 | tf_op jit(solution)/shard_map/ppermute | solution.py:20
  16.5 6.2 %collective-permute-done = f32[1,256,512]{2,1,0:T(8,128)S(1)} collective-permute-done((f32[1,256,512]{2,1,0:T(8,128)S(1)}, f32[1,256,512]{2,1,0:T(8,128)S(1)}, u32[]{:S(2)}, u32[]{:S(2)}) %collective-permute-start) | collective-permute-done | bytes 524320 | tf_op jit(solution)/shard_map/ppermute | solution.py:18
  22.7 2.4 collective-permute-done.1
  25.1 9.9 %multiply_add_fusion.3 = f32[8,256,512]{2,1,0:T(8,128)S(1)} fusion(f32[8,256,512]{2,1,0:T(8,128)} %param.3, f32[1,256,512]{2,1,0:T(8,128)S(1)} %collective-permute-done.1, f32[1,256,512]{2,1,0:T(8,128)S(1)} %collective-permute-done), kind=kLoop, calls=%fused_computation.19 | loop fusion | flops 28311552 | bytes 9437184 | tf_op jit(solution)/shard_map/add | solution.py:36
  35.1 0.1 fusion.15
  35.1 3.7 collective-permute-start.2
  38.8 4.4 collective-permute-start.3
  43.3 7.8 %collective-permute-done.2 = f32[1,256,512]{2,1,0:T(8,128)S(1)} collective-permute-done((f32[1,256,512]{2,1,0:T(8,128)S(1)}, f32[1,256,512]{2,1,0:T(8,128)S(1)}, u32[]{:S(2)}, u32[]{:S(2)}) %collective-permute-start.2) | collective-permute-done | bytes 524320 | tf_op jit(solution)/shard_map/ppermute | solution.py:18
  51.0 4.5 multiply_add_fusion.2
  55.6 2.0 copy-done.1
  57.6 0.1 fusion.14
  57.7 4.6 collective-permute-start.4
  62.3 3.3 collective-permute-start.5
  65.7 0.0 all-gather.2.cloned.1.call-update
  65.7 0.0 all-reduce.7.cloned.1.call-start
  65.7 6.6 %collective-permute-done.4 = f32[1,256,512]{2,1,0:T(8,128)S(1)} collective-permute-done((f32[1,256,512]{2,1,0:T(8,128)S(1)}, f32[1,256,512]{2,1,0:T(8,128)S(1)}, u32[]{:S(2)}, u32[]{:S(2)}) %collective-permute-start.4) | collective-permute-done | bytes 524320 | tf_op jit(solution)/shard_map/ppermute | solution.py:18
  72.3 1.6 collective-permute-done.5
  73.9 9.9 %multiply_add_fusion.1 = f32[8,256,512]{2,1,0:T(8,128)S(1)} fusion(f32[8,256,512]{2,1,0:T(8,128)} %copy-done.1, f32[1,256,512]{2,1,0:T(8,128)S(1)} %collective-permute-done.5, f32[1,256,512]{2,1,0:T(8,128)S(1)} %collective-permute-done.4), kind=kLoop, calls=%fused_computation.17 | loop fusion | flops 28311552 | bytes 9437184 | tf_op jit(solution)/shard_map/add | solution.py:36
  83.8 0.1 fusion.13
  83.9 4.1 collective-permute-start.6
  88.0 4.0 collective-permute-start.7
  92.0 15.4 %collective-permute-done.6 = f32[1,256,512]{2,1,0:T(8,128)S(1)} collective-permute-done((f32[1,256,512]{2,1,0:T(8,128)S(1)}, f32[1,256,512]{2,1,0:T(8,128)S(1)}, u32[]{:S(2)}, u32[]{:S(2)}) %collective-permute-start.6) | collective-permute-done | bytes 524320 | tf_op jit(solution)/shard_map/ppermute | solution.py:18
  107.5 5.5 multiply_add_fusion
  113.0 25.6 %all-gather.2.cloned.1.call-done = f32[256,2048]{1,0:T(8,128)} async-done(((f32[16,2048]{1,0:T(8,128)}), f32[256,2048]{1,0:T(8,128)}) %all-gather.2.cloned.1.call-update) | async-done | bytes 2097168 | tf_op jit(solution)/shard_map/all_gather | solution.py:62
  138.6 4.9 fusion.17
  143.5 0.0 all-reduce.7.cloned.1.call-update
  143.5 0.2 reduce-scatter.7.cloned.1.call-start
  143.8 8.6 %convolution_bitcast_fusion = f32[256,512]{0,1:T(8,128)S(1)} fusion(f32[2048,512]{1,0:T(8,128)} %bitcast.14, f32[256,2048]{1,0:T(8,128)S(1)} %copy-done), kind=kOutput, calls=%fused_computation.20 | convolution fusion | flops 3221225472 | bytes 6815744 | tf_op jit(solution)/shard_map/dot_general | solution.py:40
  152.3 1.0 copy.10
  153.3 0.0 reduce-scatter.7.cloned.1.call-update
  153.4 0.0 all-reduce.9.cloned.1.call-start
  153.4 24.2 %all_gather.10 = f32[256,512]{1,0:T(8,128)S(1)} all-gather(f32[16,512]{1,0:T(8,128)S(1)} %copy-done.3), channel_id=1, replica_groups=mesh['pix'=16,'tm'=16] {'pix'}, dimensions={0}, use_global_device_ids=true | all-gather | bytes 557056 | tf_op jit(solution)/shard_map/all_gather | solution.py:63
  177.6 99.5 %all-reduce.7.cloned.1.call-done = f32[256,256]{1,0:T(8,128)} async-done(((f32[256,256]{1,0:T(8,128)}), f32[256,256]{1,0:T(8,128)}) %all-reduce.7.cloned.1.call-update) | async-done | bytes 262160 | tf_op jit(solution)/shard_map/psum | solution.py:68
  277.1 85.2 %reduce-scatter.7.cloned.1.call-done = f32[16,512]{1,0:T(8,128)} async-done(((f32[256,512]{1,0:T(8,128)}), f32[16,512]{1,0:T(8,128)}) %reduce-scatter.7.cloned.1.call-update) | async-done | bytes 32784 | tf_op jit(solution)/shard_map/reduce_scatter | solution.py:67
  362.3 1.1 convolution_divide_fusion
  363.5 21.5 %all_gather.11 = f32[256,512]{1,0:T(8,128)S(1)} all-gather(f32[16,512]{1,0:T(8,128)S(1)} %convolution_divide_fusion), channel_id=1, replica_groups=mesh['pix'=16,'tm'=16] {'pix'}, dimensions={0}, use_global_device_ids=true | all-gather | bytes 557056 | tf_op jit(solution)/shard_map/all_gather | solution.py:71
  385.0 1.3 fusion.19
  386.3 0.0 all-reduce.9.cloned.1.call-update
  386.3 0.0 reduce-scatter.5.cloned.1.call-start
  386.4 7.2 %fusion.18 = f32[256,2048]{1,0:T(8,128)} fusion(f32[256,512]{1,0:T(8,128)S(1)} %all_gather.11, f32[2048,512]{1,0:T(8,128)} %bitcast.15), kind=kOutput, calls=%fused_computation.33 | convolution fusion | flops 3221225472 | bytes 6815744 | tf_op jit(solution)/shard_map/dot_general | solution.py:44
  393.6 0.0 reduce-scatter.5.cloned.1.call-update
  393.6 127.1 %all-reduce.9.cloned.1.call-done = f32[256,256]{1,0:T(8,128)} async-done(((f32[256,256]{1,0:T(8,128)}), f32[256,256]{1,0:T(8,128)}) %all-reduce.9.cloned.1.call-update) | async-done | bytes 262160 | tf_op jit(solution)/shard_map/psum | solution.py:78
  520.7 1.8 fusion.8
  522.5 72.4 %reduce-scatter.5.cloned.1.call-done = f32[16,2048]{1,0:T(8,128)} async-done(((f32[256,2048]{1,0:T(8,128)}), f32[16,2048]{1,0:T(8,128)}) %reduce-scatter.5.cloned.1.call-update) | async-done | bytes 131088 | tf_op jit(solution)/shard_map/reduce_scatter | solution.py:75
  594.9 1.6 multiply_divide_fusion
  (11 shorter events, 0.0 us)
Async XLA Ops:
  7.2 131.4 %all-gather.2.cloned.1.call-start = ((), (), s32[]{:S(2)}) async-start(), calls=%async_computation.2 | async-start | bytes 2228224 | tf_op jit(solution)/shard_map/all_gather | solution.py:62
  8.5 14.2 %collective-permute-start = (f32[1,256,512]{2,1,0:T(8,128)S(1)}, f32[1,256,512]{2,1,0:T(8,128)S(1)}, u32[]{:S(2)}, u32[]{:S(2)}) collective-permute-start(f32[1,256,512]{2,1,0:T(8,128)S(1)} %get-tuple-element.12), channel_id=1, source_target_pairs={{0,16},{16,32},{32,48},{48,64},{64,80},{80,96},{96,112},{112,128},... | collective-permute-start | bytes 1572872 | tf_op jit(solution)/shard_map/ppermute | solution.py:18
  10.4 14.7 %collective-permute-start.1 = (f32[1,256,512]{2,1,0:T(8,128)S(1)}, f32[1,256,512]{2,1,0:T(8,128)S(1)}, u32[]{:S(2)}, u32[]{:S(2)}) collective-permute-start(f32[1,256,512]{2,1,0:T(8,128)S(1)} %get-tuple-element.13), channel_id=1, source_target_pairs={{16,0},{32,16},{48,32},{64,48},{80,64},{96,80},{112,96},{128,112},... | collective-permute-start | bytes 1572872 | tf_op jit(solution)/shard_map/ppermute | solution.py:20
  35.1 15.9 %collective-permute-start.2 = (f32[1,256,512]{2,1,0:T(8,128)S(1)}, f32[1,256,512]{2,1,0:T(8,128)S(1)}, u32[]{:S(2)}, u32[]{:S(2)}) collective-permute-start(f32[1,256,512]{2,1,0:T(8,128)S(1)} %get-tuple-element.10), channel_id=1, source_target_pairs={{0,16},{16,32},{32,48},{48,64},{64,80},{80,96},{96,112},{112,128},... | collective-permute-start | bytes 1572872 | tf_op jit(solution)/shard_map/ppermute | solution.py:18
  38.8 12.2 %collective-permute-start.3 = (f32[1,256,512]{2,1,0:T(8,128)S(1)}, f32[1,256,512]{2,1,0:T(8,128)S(1)}, u32[]{:S(2)}, u32[]{:S(2)}) collective-permute-start(f32[1,256,512]{2,1,0:T(8,128)S(1)} %get-tuple-element.11), channel_id=1, source_target_pairs={{16,0},{32,16},{48,32},{64,48},{80,64},{96,80},{112,96},{128,112},... | collective-permute-start | bytes 1572872 | tf_op jit(solution)/shard_map/ppermute | solution.py:20
  55.6 2.0 copy-start.1
  57.7 14.6 %collective-permute-start.4 = (f32[1,256,512]{2,1,0:T(8,128)S(1)}, f32[1,256,512]{2,1,0:T(8,128)S(1)}, u32[]{:S(2)}, u32[]{:S(2)}) collective-permute-start(f32[1,256,512]{2,1,0:T(8,128)S(1)} %get-tuple-element.8), channel_id=1, source_target_pairs={{0,16},{16,32},{32,48},{48,64},{64,80},{80,96},{96,112},{112,128},... | collective-permute-start | bytes 1572872 | tf_op jit(solution)/shard_map/ppermute | solution.py:18
  62.3 11.6 %collective-permute-start.5 = (f32[1,256,512]{2,1,0:T(8,128)S(1)}, f32[1,256,512]{2,1,0:T(8,128)S(1)}, u32[]{:S(2)}, u32[]{:S(2)}) collective-permute-start(f32[1,256,512]{2,1,0:T(8,128)S(1)} %get-tuple-element.9), channel_id=1, source_target_pairs={{16,0},{32,16},{48,32},{64,48},{80,64},{96,80},{112,96},{128,112},... | collective-permute-start | bytes 1572872 | tf_op jit(solution)/shard_map/ppermute | solution.py:20
  65.7 211.4 %all-reduce.7.cloned.1.call-start = ((), (), s32[]{:S(2)}) async-start(), calls=%async_computation.3 | async-start | bytes 524288 | tf_op jit(solution)/shard_map/psum | solution.py:68
  83.9 23.6 %collective-permute-start.6 = (f32[1,256,512]{2,1,0:T(8,128)S(1)}, f32[1,256,512]{2,1,0:T(8,128)S(1)}, u32[]{:S(2)}, u32[]{:S(2)}) collective-permute-start(f32[1,256,512]{2,1,0:T(8,128)S(1)} %get-tuple-element.6), channel_id=1, source_target_pairs={{0,16},{16,32},{32,48},{48,64},{64,80},{80,96},{96,112},{112,128},... | collective-permute-start | bytes 1572872 | tf_op jit(solution)/shard_map/ppermute | solution.py:18
  88.0 19.5 %collective-permute-start.7 = (f32[1,256,512]{2,1,0:T(8,128)S(1)}, f32[1,256,512]{2,1,0:T(8,128)S(1)}, u32[]{:S(2)}, u32[]{:S(2)}) collective-permute-start(f32[1,256,512]{2,1,0:T(8,128)S(1)} %get-tuple-element.7), channel_id=1, source_target_pairs={{16,0},{32,16},{48,32},{64,48},{80,64},{96,80},{112,96},{128,112},... | collective-permute-start | bytes 1572872 | tf_op jit(solution)/shard_map/ppermute | solution.py:20
  138.6 5.2 copy-start
  143.5 218.8 %reduce-scatter.7.cloned.1.call-start = ((), (), s32[]{:S(2)}) async-start(), calls=%async_computation.6 | async-start | bytes 557056 | tf_op jit(solution)/shard_map/reduce_scatter | solution.py:67
  143.8 9.7 %copy-start.3 = (f32[16,512]{1,0:T(8,128)S(1)}, f32[16,512]{1,0:T(8,128)}, u32[]{:S(2)}) copy-start(f32[16,512]{1,0:T(8,128)} %param.5) | copy-start | bytes 98308
  153.4 367.3 %all-reduce.9.cloned.1.call-start = ((), (), s32[]{:S(2)}) async-start(), calls=%async_computation.5 | async-start | bytes 524288 | tf_op jit(solution)/shard_map/psum | solution.py:78
  363.5 30.1 %copy-start.4 = (f32[16,512]{1,0:T(8,128)}, f32[16,512]{1,0:T(8,128)S(1)}, u32[]{:S(2)}) copy-start(f32[16,512]{1,0:T(8,128)S(1)} %convolution_divide_fusion) | copy-start | bytes 98308
  386.3 208.6 %copy-start.2 = (f32[16,2048]{1,0:T(8,128)S(1)}, f32[16,2048]{1,0:T(8,128)}, u32[]{:S(2)}) copy-start(f32[16,2048]{1,0:T(8,128)} %param.4) | copy-start | bytes 393220
  386.3 208.6 %reduce-scatter.5.cloned.1.call-start = ((), (), s32[]{:S(2)}) async-start(), calls=%async_computation.4 | async-start | bytes 2228224 | tf_op jit(solution)/shard_map/reduce_scatter | solution.py:75
Sparse Core Ops, SparseCore 0:
  65.8 72.7 all-gather.1
  143.7 133.4 all-reduce.6
  281.7 80.6 reduce-scatter.6
  386.5 134.1 all-reduce.8
  523.2 71.6 reduce-scatter.4
where the time goes:
time: 604 us; the launch traced here: 603 us
  waiting for transfers between devices  450 us (75%)
  blocking collectives  45.7 us (8%)
  starting transfers between devices  32.6 us (5%)
  other arithmetic  31.4 us (5%)
  matrix products  24.9 us (4%)
  between operations  14 us (2%)
    psum x1, waiting for transfers between devices, body(): trace_gram = lax.psum(contract_last(new_full, new_full), 'tm')  127 us
    psum x1, waiting for transfers between devices, body(): gram = lax.psum(contract_last(foot_full, foot_full), 'pix')  99.5 us
    reduce_scatter x1, waiting for transfers between devices, body(): lax.psum_scatter(matmul_hi(part, pixels), 'pix', scatter_dimension=0, til...  85.2 us
    reduce_scatter x1, waiting for transfers between devices, body(): lax.psum_scatter(contract_last(part, pixels), 'tm', scatter_dimension=0,...  72.4 us
    ppermute x4, waiting for transfers between devices, with_halo(): lax.ppermute(tail, axis, [(i, (i + 1) % count) for i in range(ends)])  36 us
    add x4, other arithmetic, substep(): return middle + step_size * summed  29.8 us
    all_gather x1, waiting for transfers between devices, body(): foot_full = lax.all_gather(footprints, 'tm', axis=0, tiled=True)  25.6 us
    all_gather x1, blocking collectives, body(): trace_full = lax.all_gather(traces, 'pix', axis=0, tiled=True)  24.2 us
  transfers between devices with their start and end apart: 13, of which 11 were waited for; matrix products, arithmetic and copies ran while one was open for 6% of the time, Pallas kernels for 0%

commit v1 on v0

--- a/solution.py
+++ b/solution.py
@@ -75,7 +75,8 @@
     foot_numerator = lax.psum_scatter(
         contract_last(part, pixels), "tm", scatter_dimension=0, tiled=True
     )
-    trace_gram = lax.psum(contract_last(new_full, new_full), "tm")
+    q_in = contract_last(new_full, new_full)
+    trace_gram = lax.all_gather(q_in, axis_name="tm").sum(axis=0)
     trace_rows = lax.dynamic_slice_in_dim(trace_gram, foot_start, foot_block, 0)
     new_footprints = footprints * foot_numerator / matmul_hi(trace_rows, foot_full)
     return (current, new_footprints, new_traces)

time: 604 us -> 546 us (0.904)
  waiting for transfers between devices: 450 us -> 391 us
    psum x1 -> x0, waiting for transfers between devices: 127 us -> none  [body(): trace_gram = lax.psum(contract_last(new_full, new_full), 'tm')]
    all_gather x0 -> x1, waiting for transfers between devices: none -> 69.6 us  [body(): trace_gram = lax.all_gather(q_in, axis_name='tm').sum(axis=0)]
  transfers between devices with their start and end apart: 13 -> 13, of which waited for: 11 -> 11; matrix products, arithmetic and copies ran while one was open for 6% -> 7% of each run, Pallas kernels for 0% -> 0%
where the time goes in v1:
time: 546 us; the launch traced here: 545 us
  waiting for transfers between devices  391 us (72%)
  blocking collectives  45.6 us (8%)
  other arithmetic  33.9 us (6%)
  starting transfers between devices  32.6 us (6%)
  matrix products  24.2 us (4%)
  between operations  14 us (3%)
    psum x1, waiting for transfers between devices, body(): gram = lax.psum(contract_last(foot_full, foot_full), 'pix')  99.7 us
    reduce_scatter x1, waiting for transfers between devices, body(): lax.psum_scatter(matmul_hi(part, pixels), 'pix', scatter_dimension=0, til...  85.2 us
    reduce_scatter x1, waiting for transfers between devices, body(): lax.psum_scatter(contract_last(part, pixels), 'tm', scatter_dimension=0,...  70.6 us
    all_gather x1, waiting for transfers between devices, body(): trace_gram = lax.all_gather(q_in, axis_name='tm').sum(axis=0)  69.6 us
    ppermute x4, waiting for transfers between devices, with_halo(): lax.ppermute(tail, axis, [(i, (i + 1) % count) for i in range(ends)])  36.1 us
    add x4, other arithmetic, substep(): return middle + step_size * summed  29.9 us
    all_gather x1, waiting for transfers between devices, body(): foot_full = lax.all_gather(footprints, 'tm', axis=0, tiled=True)  25.4 us
    all_gather x1, blocking collectives, body(): trace_full = lax.all_gather(traces, 'pix', axis=0, tiled=True)  24.2 us
  transfers between devices with their start and end apart: 13, of which 11 were waited for; matrix products, arithmetic and copies ran while one was open for 7% of the time, Pallas kernels for 0%

profile of v1, /device:TPU:8, one launch (start us, length us, event | category | flops | bytes accessed | tf_op | source)
XLA Modules:
  0.0 545.5 jit_solution(16281174521953557911)
XLA Ops:
  7.2 0.0 all-gather.4.cloned.1.call-start
  7.2 1.3 fusion.16
  8.5 1.9 collective-permute-start
  10.4 6.0 %collective-permute-start.1 = (f32[1,256,512]{2,1,0:T(8,128)S(1)}, f32[1,256,512]{2,1,0:T(8,128)S(1)}, u32[]{:S(2)}, u32[]{:S(2)}) collective-permute-start(f32[1,256,512]{2,1,0:T(8,128)S(1)} %get-tuple-element.13), channel_id=1, source_target_pairs={{16,0},{32,16},{48,32},{64,48},{80,64},{96,80},{112,96},{128,112},... | collective-permute-start | bytes 1572872 | tf_op jit(solution)/shard_map/ppermute | solution.py:20
  16.5 6.2 %collective-permute-done = f32[1,256,512]{2,1,0:T(8,128)S(1)} collective-permute-done((f32[1,256,512]{2,1,0:T(8,128)S(1)}, f32[1,256,512]{2,1,0:T(8,128)S(1)}, u32[]{:S(2)}, u32[]{:S(2)}) %collective-permute-start) | collective-permute-done | bytes 524320 | tf_op jit(solution)/shard_map/ppermute | solution.py:18
  22.7 2.4 collective-permute-done.1
  25.1 9.8 %multiply_add_fusion.3 = f32[8,256,512]{2,1,0:T(8,128)S(1)} fusion(f32[8,256,512]{2,1,0:T(8,128)} %param.3, f32[1,256,512]{2,1,0:T(8,128)S(1)} %collective-permute-done.1, f32[1,256,512]{2,1,0:T(8,128)S(1)} %collective-permute-done), kind=kLoop, calls=%fused_computation.19 | loop fusion | flops 28311552 | bytes 9437184 | tf_op jit(solution)/shard_map/add | solution.py:36
  35.0 0.1 fusion.15
  35.1 3.7 collective-permute-start.2
  38.8 4.4 collective-permute-start.3
  43.2 7.8 %collective-permute-done.2 = f32[1,256,512]{2,1,0:T(8,128)S(1)} collective-permute-done((f32[1,256,512]{2,1,0:T(8,128)S(1)}, f32[1,256,512]{2,1,0:T(8,128)S(1)}, u32[]{:S(2)}, u32[]{:S(2)}) %collective-permute-start.2) | collective-permute-done | bytes 524320 | tf_op jit(solution)/shard_map/ppermute | solution.py:18
  51.0 4.5 multiply_add_fusion.2
  55.5 2.0 copy-done.1
  57.5 0.1 fusion.14
  57.6 4.6 collective-permute-start.4
  62.2 3.3 collective-permute-start.5
  65.6 0.0 all-gather.4.cloned.1.call-update
  65.6 0.0 all-reduce.6.cloned.1.call-start
  65.7 6.6 %collective-permute-done.4 = f32[1,256,512]{2,1,0:T(8,128)S(1)} collective-permute-done((f32[1,256,512]{2,1,0:T(8,128)S(1)}, f32[1,256,512]{2,1,0:T(8,128)S(1)}, u32[]{:S(2)}, u32[]{:S(2)}) %collective-permute-start.4) | collective-permute-done | bytes 524320 | tf_op jit(solution)/shard_map/ppermute | solution.py:18
  72.3 1.6 collective-permute-done.5
  73.9 10.0 %multiply_add_fusion.1 = f32[8,256,512]{2,1,0:T(8,128)S(1)} fusion(f32[8,256,512]{2,1,0:T(8,128)} %copy-done.1, f32[1,256,512]{2,1,0:T(8,128)S(1)} %collective-permute-done.5, f32[1,256,512]{2,1,0:T(8,128)S(1)} %collective-permute-done.4), kind=kLoop, calls=%fused_computation.17 | loop fusion | flops 28311552 | bytes 9437184 | tf_op jit(solution)/shard_map/add | solution.py:36
  83.9 0.1 fusion.13
  83.9 4.1 collective-permute-start.6
  88.1 4.0 collective-permute-start.7
  92.1 15.5 %collective-permute-done.6 = f32[1,256,512]{2,1,0:T(8,128)S(1)} collective-permute-done((f32[1,256,512]{2,1,0:T(8,128)S(1)}, f32[1,256,512]{2,1,0:T(8,128)S(1)}, u32[]{:S(2)}, u32[]{:S(2)}) %collective-permute-start.6) | collective-permute-done | bytes 524320 | tf_op jit(solution)/shard_map/ppermute | solution.py:18
  107.6 5.5 %multiply_add_fusion = f32[8,256,512]{2,1,0:T(8,128)} fusion(f32[8,256,512]{2,1,0:T(8,128)S(1)} %multiply_add_fusion.1, f32[1,256,512]{2,1,0:T(8,128)S(1)} %collective-permute-done.7, f32[1,256,512]{2,1,0:T(8,128)S(1)} %collective-permute-done.6), kind=kLoop, calls=%fused_computation.16 | loop fusion | flops 28311552 | bytes 9437184 | tf_op jit(solution)/shard_map/add | solution.py:36
  113.1 25.4 %all-gather.4.cloned.1.call-done = f32[256,2048]{1,0:T(8,128)} async-done(((f32[16,2048]{1,0:T(8,128)}), f32[256,2048]{1,0:T(8,128)}) %all-gather.4.cloned.1.call-update) | async-done | bytes 2097168 | tf_op jit(solution)/shard_map/all_gather | solution.py:62
  138.5 4.9 fusion.17
  143.4 0.0 all-reduce.6.cloned.1.call-update
  143.5 0.2 reduce-scatter.7.cloned.1.call-start
  143.7 8.6 %convolution_bitcast_fusion = f32[256,512]{0,1:T(8,128)S(1)} fusion(f32[2048,512]{1,0:T(8,128)} %bitcast.15, f32[256,2048]{1,0:T(8,128)S(1)} %copy-done), kind=kOutput, calls=%fused_computation.20 | convolution fusion | flops 3221225472 | bytes 6815744 | tf_op jit(solution)/shard_map/dot_general | solution.py:40
  152.3 1.0 copy.10
  153.3 0.0 reduce-scatter.7.cloned.1.call-update
  153.3 0.0 all-gather.6.cloned.1.call-start
  153.4 24.2 %all_gather.16 = f32[256,512]{1,0:T(8,128)S(1)} all-gather(f32[16,512]{1,0:T(8,128)S(1)} %copy-done.3), channel_id=1, replica_groups=mesh['pix'=16,'tm'=16] {'pix'}, dimensions={0}, use_global_device_ids=true | all-gather | bytes 557056 | tf_op jit(solution)/shard_map/all_gather | solution.py:63
  177.5 99.7 %all-reduce.6.cloned.1.call-done = f32[256,256]{1,0:T(8,128)} async-done(((f32[256,256]{1,0:T(8,128)}), f32[256,256]{1,0:T(8,128)}) %all-reduce.6.cloned.1.call-update) | async-done | bytes 262160 | tf_op jit(solution)/shard_map/psum | solution.py:68
  277.2 85.2 %reduce-scatter.7.cloned.1.call-done = f32[16,512]{1,0:T(8,128)} async-done(((f32[256,512]{1,0:T(8,128)}), f32[16,512]{1,0:T(8,128)}) %reduce-scatter.7.cloned.1.call-update) | async-done | bytes 32784 | tf_op jit(solution)/shard_map/reduce_scatter | solution.py:67
  362.4 1.1 convolution_divide_fusion
  363.5 21.5 %all_gather.17 = f32[256,512]{1,0:T(8,128)S(1)} all-gather(f32[16,512]{1,0:T(8,128)S(1)} %convolution_divide_fusion), channel_id=1, replica_groups=mesh['pix'=16,'tm'=16] {'pix'}, dimensions={0}, use_global_device_ids=true | all-gather | bytes 557056 | tf_op jit(solution)/shard_map/all_gather | solution.py:71
  385.0 1.3 fusion.19
  386.4 0.0 reduce-scatter.5.cloned.1.call-start
  386.4 7.2 %fusion.18 = f32[256,2048]{1,0:T(8,128)} fusion(f32[256,512]{1,0:T(8,128)S(1)} %all_gather.17, f32[2048,512]{1,0:T(8,128)} %bitcast.16), kind=kOutput, calls=%fused_computation.33 | convolution fusion | flops 3221225472 | bytes 6815744 | tf_op jit(solution)/shard_map/dot_general | solution.py:44
  393.6 0.0 reduce-scatter.5.cloned.1.call-update
  393.7 69.6 %all-gather.6.cloned.1.call-done = f32[4096,256]{1,0:T(8,128)} async-done(((f32[256,256]{1,0:T(8,128)}), f32[4096,256]{1,0:T(8,128)}) %all-gather.6.cloned.1.call-update) | async-done | bytes 4194320 | tf_op jit(solution)/shard_map/all_gather | solution.py:79
  463.2 2.5 reduce_sum.9
  465.7 1.1 fusion.8
  466.8 70.6 %reduce-scatter.5.cloned.1.call-done = f32[16,2048]{1,0:T(8,128)} async-done(((f32[256,2048]{1,0:T(8,128)}), f32[16,2048]{1,0:T(8,128)}) %reduce-scatter.5.cloned.1.call-update) | async-done | bytes 131088 | tf_op jit(solution)/shard_map/reduce_scatter | solution.py:75
  537.4 1.6 multiply_divide_fusion
  (12 shorter events, 0.0 us)
Async XLA Ops:
  7.2 131.3 %all-gather.4.cloned.1.call-start = ((), (), s32[]{:S(2)}) async-start(), calls=%async_computation.2 | async-start | bytes 2228224 | tf_op jit(solution)/shard_map/all_gather | solution.py:62
  8.5 14.2 %collective-permute-start = (f32[1,256,512]{2,1,0:T(8,128)S(1)}, f32[1,256,512]{2,1,0:T(8,128)S(1)}, u32[]{:S(2)}, u32[]{:S(2)}) collective-permute-start(f32[1,256,512]{2,1,0:T(8,128)S(1)} %get-tuple-element.12), channel_id=1, source_target_pairs={{0,16},{16,32},{32,48},{48,64},{64,80},{80,96},{96,112},{112,128},... | collective-permute-start | bytes 1572872 | tf_op jit(solution)/shard_map/ppermute | solution.py:18
  10.4 14.7 %collective-permute-start.1 = (f32[1,256,512]{2,1,0:T(8,128)S(1)}, f32[1,256,512]{2,1,0:T(8,128)S(1)}, u32[]{:S(2)}, u32[]{:S(2)}) collective-permute-start(f32[1,256,512]{2,1,0:T(8,128)S(1)} %get-tuple-element.13), channel_id=1, source_target_pairs={{16,0},{32,16},{48,32},{64,48},{80,64},{96,80},{112,96},{128,112},... | collective-permute-start | bytes 1572872 | tf_op jit(solution)/shard_map/ppermute | solution.py:20
  35.1 15.9 %collective-permute-start.2 = (f32[1,256,512]{2,1,0:T(8,128)S(1)}, f32[1,256,512]{2,1,0:T(8,128)S(1)}, u32[]{:S(2)}, u32[]{:S(2)}) collective-permute-start(f32[1,256,512]{2,1,0:T(8,128)S(1)} %get-tuple-element.10), channel_id=1, source_target_pairs={{0,16},{16,32},{32,48},{48,64},{64,80},{80,96},{96,112},{112,128},... | collective-permute-start | bytes 1572872 | tf_op jit(solution)/shard_map/ppermute | solution.py:18
  38.8 12.2 %collective-permute-start.3 = (f32[1,256,512]{2,1,0:T(8,128)S(1)}, f32[1,256,512]{2,1,0:T(8,128)S(1)}, u32[]{:S(2)}, u32[]{:S(2)}) collective-permute-start(f32[1,256,512]{2,1,0:T(8,128)S(1)} %get-tuple-element.11), channel_id=1, source_target_pairs={{16,0},{32,16},{48,32},{64,48},{80,64},{96,80},{112,96},{128,112},... | collective-permute-start | bytes 1572872 | tf_op jit(solution)/shard_map/ppermute | solution.py:20
  55.5 2.0 copy-start.1
  57.6 14.6 %collective-permute-start.4 = (f32[1,256,512]{2,1,0:T(8,128)S(1)}, f32[1,256,512]{2,1,0:T(8,128)S(1)}, u32[]{:S(2)}, u32[]{:S(2)}) collective-permute-start(f32[1,256,512]{2,1,0:T(8,128)S(1)} %get-tuple-element.8), channel_id=1, source_target_pairs={{0,16},{16,32},{32,48},{48,64},{64,80},{80,96},{96,112},{112,128},... | collective-permute-start | bytes 1572872 | tf_op jit(solution)/shard_map/ppermute | solution.py:18
  62.2 11.6 %collective-permute-start.5 = (f32[1,256,512]{2,1,0:T(8,128)S(1)}, f32[1,256,512]{2,1,0:T(8,128)S(1)}, u32[]{:S(2)}, u32[]{:S(2)}) collective-permute-start(f32[1,256,512]{2,1,0:T(8,128)S(1)} %get-tuple-element.9), channel_id=1, source_target_pairs={{16,0},{32,16},{48,32},{64,48},{80,64},{96,80},{112,96},{128,112},... | collective-permute-start | bytes 1572872 | tf_op jit(solution)/shard_map/ppermute | solution.py:20
  65.6 211.6 %all-reduce.6.cloned.1.call-start = ((), (), s32[]{:S(2)}) async-start(), calls=%async_computation.3 | async-start | bytes 524288 | tf_op jit(solution)/shard_map/psum | solution.py:68
  83.9 23.6 %collective-permute-start.6 = (f32[1,256,512]{2,1,0:T(8,128)S(1)}, f32[1,256,512]{2,1,0:T(8,128)S(1)}, u32[]{:S(2)}, u32[]{:S(2)}) collective-permute-start(f32[1,256,512]{2,1,0:T(8,128)S(1)} %get-tuple-element.6), channel_id=1, source_target_pairs={{0,16},{16,32},{32,48},{48,64},{64,80},{80,96},{96,112},{112,128},... | collective-permute-start | bytes 1572872 | tf_op jit(solution)/shard_map/ppermute | solution.py:18
  88.1 19.5 %collective-permute-start.7 = (f32[1,256,512]{2,1,0:T(8,128)S(1)}, f32[1,256,512]{2,1,0:T(8,128)S(1)}, u32[]{:S(2)}, u32[]{:S(2)}) collective-permute-start(f32[1,256,512]{2,1,0:T(8,128)S(1)} %get-tuple-element.7), channel_id=1, source_target_pairs={{16,0},{32,16},{48,32},{64,48},{80,64},{96,80},{112,96},{128,112},... | collective-permute-start | bytes 1572872 | tf_op jit(solution)/shard_map/ppermute | solution.py:20
  138.5 5.2 copy-start
  143.5 218.9 %reduce-scatter.7.cloned.1.call-start = ((), (), s32[]{:S(2)}) async-start(), calls=%async_computation.6 | async-start | bytes 557056 | tf_op jit(solution)/shard_map/reduce_scatter | solution.py:67
  143.7 9.7 %copy-start.3 = (f32[16,512]{1,0:T(8,128)S(1)}, f32[16,512]{1,0:T(8,128)}, u32[]{:S(2)}) copy-start(f32[16,512]{1,0:T(8,128)} %param.5) | copy-start | bytes 98308
  153.3 309.9 %all-gather.6.cloned.1.call-start = ((), (), s32[]{:S(2)}) async-start(), calls=%async_computation.5 | async-start | bytes 4456448 | tf_op jit(solution)/shard_map/all_gather | solution.py:79
  363.5 30.1 %copy-start.4 = (f32[16,512]{1,0:T(8,128)}, f32[16,512]{1,0:T(8,128)S(1)}, u32[]{:S(2)}) copy-start(f32[16,512]{1,0:T(8,128)S(1)} %convolution_divide_fusion) | copy-start | bytes 98308
  386.4 151.0 %reduce-scatter.5.cloned.1.call-start = ((), (), s32[]{:S(2)}) async-start(), calls=%async_computation.4 | async-start | bytes 2228224 | tf_op jit(solution)/shard_map/reduce_scatter | solution.py:75
  393.6 143.7 %copy-start.2 = (f32[16,2048]{1,0:T(8,128)S(1)}, f32[16,2048]{1,0:T(8,128)}, u32[]{:S(2)}) copy-start(f32[16,2048]{1,0:T(8,128)} %param.4) | copy-start | bytes 393220
Sparse Core Ops, SparseCore 0:
  65.7 72.7 all-gather.3
  143.6 133.5 all-reduce.5
  281.7 80.6 reduce-scatter.6
  386.5 76.6 all-gather.5
  465.6 71.7 reduce-scatter.4
